TPU v7x, 32 devices: a whole 2x2x4 slice. The times are simulated.
32 devices in a mesh: ctx: 4 (over y, core), exp: 8 (over z, x).
Axes of the slice: x: 2, y: 2, z: 4, core: 2. Of those that a mesh axis runs over, the one named last changes fastest.
Arguments:
- layer_input: bfloat16 [8, 1536, 2048], P('exp', 'ctx'), may hold values from -30 to 30
- block_ids: int32 [8, 8], P('exp'), may hold values from 0 to 7, as said below
- routes: int32 [8, 1536, 8], P('exp', 'ctx'), may hold values from 0 to 15, all different within a row
- w_query: bfloat16 [2048, 2048], P('exp'), may hold values from -0.125 to 0.125
- w_key: bfloat16 [2048, 2048], P('exp'), may hold values from -0.125 to 0.125
- w_value: bfloat16 [2048, 2048], P('exp'), may hold values from -0.125 to 0.125
- w_output: bfloat16 [2048, 2048], P('exp'), may hold values from -2 to 2
- w_router: bfloat16 [2048, 16], P('exp'), may hold values from -0.0625 to 0.0625
- norm_gains: bfloat16 [2048, 4], P('exp'), may hold values from 0.25 to 1.75
- w_gate_up: bfloat16 [16, 4096, 1024], P('exp', None, 'ctx'), may hold values from -0.125 to 0.125
- w_down: bfloat16 [16, 2048, 1024], P('exp', None, 'ctx'), may hold values from -4 to 4
- d_out: bfloat16 [8, 1536, 2048], P('exp', 'ctx'), may hold values from -6 to 6
Outputs:
- output: bfloat16 [8, 1536, 2048], P('exp', 'ctx')
- d_x: float32 [8, 1536, 2048], P('exp', 'ctx')
- g_query: float32 [2048, 2048], P('exp')
- g_key: float32 [2048, 2048], P('exp')
- g_value: float32 [2048, 2048], P('exp')
- g_output: float32 [2048, 2048], P('exp')
- g_router: float32 [2048, 16], P('exp')
- g_gains: float32 [2048, 4], P('exp')
- g_gate_up: float32 [16, 4096, 1024], P('exp', None, 'ctx')
- g_down: float32 [16, 2048, 1024], P('exp', None, 'ctx')
Inputs may be any that keep to these rules, and one draw needn't show every extreme that they name: `block_ids`: each row holds each block number once; the two blocks of one device add up to 7. `routes`: each token names 8 different experts.
All inputs are finite; a program needn't handle non-finite values.
Results may differ from a plain program's by a relative error of at most 0.025.
Values may be sent and summed in bfloat16 or wider, within the bound.
A program may use at most 448 MiB of HBM per device.

v0:
```python
import jax
import jax.numpy as jnp
from jax import lax
from jax.sharding import PartitionSpec as P

HEAD_DIM = 128
epsilon = 1e-05
rope_theta = 10000.0


def rms_scale(matrix, gain):
    return matrix * lax.rsqrt(jnp.mean(matrix * matrix, axis=-1, keepdims=True) + epsilon) * gain


def angle_tables(positions, head_width):
    half_width = head_width // 2
    inverse = rope_theta ** (-(jnp.arange(half_width, dtype=jnp.float32) * 2.0) / head_width)
    angles = positions.astype(jnp.float32)[:, None] * inverse[None, :]
    angles = jnp.concatenate([angles, angles], axis=-1)
    return (jnp.cos(angles), jnp.sin(angles))


def rotate(matrix, cosine, sine, head_count, head_width):
    row_count = matrix.shape[0]
    split_heads = matrix.reshape(row_count, head_count, head_width)
    half_width = head_width // 2
    turned = jnp.concatenate(
        [-split_heads[..., half_width:], split_heads[..., :half_width]], axis=-1
    )
    result = split_heads * cosine[:, None, :] + turned * sine[:, None, :]
    return result.reshape(row_count, head_count * head_width)


def all_positions(block_row, half_rows):
    offsets = jnp.arange(half_rows, dtype=jnp.int32)
    return (block_row[:, None] * half_rows + offsets[None, :]).reshape(-1)


def slot_table(route_rows, expert_count, capacity):
    flat_routes = route_rows.reshape(-1)
    onehot = (flat_routes[:, None] == jnp.arange(expert_count, dtype=jnp.int32)[None, :]).astype(
        jnp.int32
    )
    rank_of = jnp.sum(jnp.cumsum(onehot, axis=0) * onehot, axis=1) - 1
    kept_mask = rank_of < capacity
    pair_slot = jnp.where(kept_mask, flat_routes * capacity + rank_of, expert_count * capacity)
    return (pair_slot, kept_mask)


def per_device(
    layer_input,
    block_ids,
    routes,
    w_query,
    w_key,
    w_value,
    w_output,
    w_router,
    norm_gains,
    w_gate_up,
    w_down,
    d_out,
):
    query_full, key_full, value_full, output_full, router_full, gains_bf = (
        lax.all_gather(w_query, "exp", axis=0, tiled=True),
        lax.all_gather(w_key, "exp", axis=0, tiled=True),
        lax.all_gather(w_value, "exp", axis=0, tiled=True),
        lax.all_gather(w_output, "exp", axis=0, tiled=True),
        lax.all_gather(w_router, "exp", axis=0, tiled=True),
        lax.all_gather(norm_gains, "exp", axis=0, tiled=True),
    )
    gain_table = gains_bf.astype(jnp.float32)
    tokens = layer_input[0].astype(jnp.float32)
    row_count, model_width = tokens.shape
    head_width = HEAD_DIM
    head_count = model_width // head_width
    half_rows = row_count // 2
    key_positions = all_positions(block_ids[0], half_rows)
    device_index = lax.axis_index("ctx")
    query_positions = lax.dynamic_slice_in_dim(key_positions, device_index * row_count, row_count)
    cosine, sine = angle_tables(query_positions, head_width)
    score_scale = head_width ** (-0.5)

    def norm_rope(projected, gain):
        return rotate(rms_scale(projected, gain), cosine, sine, head_count, head_width)

    first_norm = rms_scale(tokens, gain_table[:, 0]).astype(jnp.bfloat16)
    query_pre = jnp.dot(first_norm, query_full, preferred_element_type=jnp.float32)
    key_pre = jnp.dot(first_norm, key_full, preferred_element_type=jnp.float32)
    own_values = jnp.dot(first_norm, value_full, preferred_element_type=jnp.float32).astype(
        jnp.bfloat16
    )
    query = norm_rope(query_pre, gain_table[:, 1]).astype(jnp.bfloat16)
    own_keys = norm_rope(key_pre, gain_table[:, 2]).astype(jnp.bfloat16)
    all_keys, all_values = (
        lax.all_gather(own_keys, "ctx", axis=0, tiled=True),
        lax.all_gather(own_values, "ctx", axis=0, tiled=True),
    )
    seq_length = all_keys.shape[0]
    query_heads = query.reshape(row_count, head_count, head_width)
    key_heads = all_keys.reshape(seq_length, head_count, head_width)
    value_heads = all_values.reshape(seq_length, head_count, head_width)
    visible = key_positions[None, :] <= query_positions[:, None]

    def scores_of():
        raw_scores = (
            jnp.einsum("qhd,khd->hqk", query_heads, key_heads, preferred_element_type=jnp.float32)
            * score_scale
        )
        return jnp.where(visible[None], raw_scores, -1e30)

    scores = scores_of()
    top_score = jnp.max(scores, axis=-1, keepdims=True)
    log_total = top_score + jnp.log(jnp.sum(jnp.exp(scores - top_score), axis=-1, keepdims=True))
    probs_low = jnp.exp(scores - log_total).astype(jnp.bfloat16)
    attended = (
        jnp.einsum("hqk,khd->qhd", probs_low, value_heads, preferred_element_type=jnp.float32)
        .reshape(row_count, model_width)
        .astype(jnp.bfloat16)
    )
    hidden = tokens + jnp.dot(attended, output_full, preferred_element_type=jnp.float32)
    second_norm = rms_scale(hidden, gain_table[:, 3]).astype(jnp.bfloat16)
    logits = jnp.dot(second_norm, router_full, preferred_element_type=jnp.float32)
    router_probs = jax.nn.softmax(logits, axis=-1)
    expert_count = router_full.shape[1]
    route_rows = routes[0]
    top_count = route_rows.shape[1]
    chosen_mask = (
        route_rows[..., None] == jnp.arange(expert_count, dtype=jnp.int32)[None, None, :]
    ).astype(jnp.float32)
    gates = jnp.sum(chosen_mask * router_probs[:, None, :], axis=-1)
    capacity = (5 * row_count * top_count + 4 * expert_count - 1) // (4 * expert_count)
    pair_slot, kept_mask = slot_table(route_rows, expert_count, capacity)
    slot_total = expert_count * capacity
    pair_rows = jnp.repeat(second_norm, top_count, axis=0)
    send_rows = jnp.zeros((slot_total + 1, model_width), jnp.bfloat16).at[pair_slot].set(pair_rows)
    send_rows = send_rows[:slot_total].reshape(expert_count, capacity, model_width)
    arrived = lax.all_to_all(send_rows, "exp", split_axis=0, concat_axis=1, tiled=True)
    gate_up_full, down_full = (
        lax.all_gather(w_gate_up, "ctx", axis=2, tiled=True),
        lax.all_gather(w_down, "ctx", axis=2, tiled=True),
    )
    gate_full = gate_up_full[:, :model_width]
    up_full = gate_up_full[:, model_width:]
    gate_pre = jnp.einsum("erd,edf->erf", arrived, gate_full, preferred_element_type=jnp.float32)
    up_pre = jnp.einsum("erd,edf->erf", arrived, up_full, preferred_element_type=jnp.float32)
    activated = jax.nn.silu(gate_pre)
    inner = (activated * up_pre).astype(jnp.bfloat16)
    expert_out = jnp.einsum(
        "erf,edf->erd", inner, down_full, preferred_element_type=jnp.float32
    ).astype(jnp.bfloat16)
    returned = lax.all_to_all(expert_out, "exp", split_axis=1, concat_axis=0, tiled=True)
    padded_out = jnp.concatenate(
        [returned.reshape(slot_total, model_width), jnp.zeros((1, model_width), jnp.bfloat16)],
        axis=0,
    )
    pair_out = padded_out[pair_slot].astype(jnp.float32).reshape(row_count, top_count, model_width)
    mixture = jnp.sum(gates[..., None] * pair_out, axis=1)
    output = (hidden + mixture).astype(jnp.bfloat16)[None]
    grad_out = d_out[0].astype(jnp.float32)
    pair_weight = jnp.where(kept_mask, gates.reshape(-1), 0.0)
    pair_grad = (pair_weight[:, None] * jnp.repeat(grad_out, top_count, axis=0)).astype(
        jnp.bfloat16
    )
    send_grad = jnp.zeros((slot_total + 1, model_width), jnp.bfloat16).at[pair_slot].set(pair_grad)
    send_grad = send_grad[:slot_total].reshape(expert_count, capacity, model_width)
    gate_grad = jnp.sum(pair_out * grad_out[:, None, :], axis=-1)
    out_grad = lax.all_to_all(send_grad, "exp", split_axis=0, concat_axis=1, tiled=True)
    gate_up_again, down_back = (
        lax.all_gather(w_gate_up, "ctx", axis=2, tiled=True),
        lax.all_gather(w_down, "ctx", axis=2, tiled=True),
    )
    gate_back = gate_up_again[:, :model_width]
    up_back = gate_up_again[:, model_width:]
    inner_grad = jnp.einsum("erd,edf->erf", out_grad, down_back, preferred_element_type=jnp.float32)
    sigmoid_gate = jax.nn.sigmoid(gate_pre)
    gate_pre_grad = (
        inner_grad * up_pre * sigmoid_gate * (1.0 + gate_pre * (1.0 - sigmoid_gate))
    ).astype(jnp.bfloat16)
    up_pre_grad = (inner_grad * activated).astype(jnp.bfloat16)
    down_grad = jnp.einsum("erd,erf->edf", out_grad, inner, preferred_element_type=jnp.float32)
    gate_w_grad = jnp.einsum(
        "erd,erf->edf", arrived, gate_pre_grad, preferred_element_type=jnp.float32
    )
    up_w_grad = jnp.einsum("erd,erf->edf", arrived, up_pre_grad, preferred_element_type=jnp.float32)
    arrived_grad = jnp.einsum(
        "erf,edf->erd", gate_pre_grad, gate_back, preferred_element_type=jnp.float32
    )
    arrived_grad = (
        arrived_grad
        + jnp.einsum("erf,edf->erd", up_pre_grad, up_back, preferred_element_type=jnp.float32)
    ).astype(jnp.bfloat16)
    gate_up_grad, down_grad_shard = (
        lax.psum_scatter(
            jnp.concatenate([gate_w_grad, up_w_grad], axis=1).astype(jnp.bfloat16),
            "ctx",
            scatter_dimension=2,
            tiled=True,
        ).astype(jnp.float32),
        lax.psum_scatter(
            down_grad.astype(jnp.bfloat16), "ctx", scatter_dimension=2, tiled=True
        ).astype(jnp.float32),
    )
    back_rows = lax.all_to_all(arrived_grad, "exp", split_axis=1, concat_axis=0, tiled=True)
    padded_back = jnp.concatenate(
        [back_rows.reshape(slot_total, model_width), jnp.zeros((1, model_width), jnp.bfloat16)],
        axis=0,
    )
    second_grad = jnp.sum(
        padded_back[pair_slot].astype(jnp.float32).reshape(row_count, top_count, model_width),
        axis=1,
    )
    prob_grad = jnp.sum(chosen_mask * gate_grad[..., None], axis=1)
    logit_grad = (
        router_probs * (prob_grad - jnp.sum(prob_grad * router_probs, axis=-1, keepdims=True))
    ).astype(jnp.bfloat16)
    second_grad = second_grad + jnp.einsum(
        "te,de->td", logit_grad, router_full, preferred_element_type=jnp.float32
    )
    second_value, second_back = jax.vjp(rms_scale, hidden, gain_table[:, 3])
    hidden_part, gain_two_grad = second_back(second_grad)
    hidden_grad = grad_out + hidden_part
    hidden_grad_low = hidden_grad.astype(jnp.bfloat16)
    attended_grad = jnp.einsum(
        "tf,df->td", hidden_grad_low, output_full, preferred_element_type=jnp.float32
    ).astype(jnp.bfloat16)
    attended_heads = attended_grad.reshape(row_count, head_count, head_width)
    probs_again = jnp.exp(scores_of() - log_total)
    probs_grad = jnp.einsum(
        "qhd,khd->hqk", attended_heads, value_heads, preferred_element_type=jnp.float32
    )
    row_dot = jnp.sum(probs_again * probs_grad, axis=-1, keepdims=True)
    score_grad = (probs_again * (probs_grad - row_dot)).astype(jnp.bfloat16)
    query_grad = (
        jnp.einsum(
            "hqk,khd->qhd", score_grad, key_heads, preferred_element_type=jnp.float32
        ).reshape(row_count, model_width)
        * score_scale
    )
    key_part = (
        jnp.einsum(
            "hqk,qhd->khd", score_grad, query_heads, preferred_element_type=jnp.float32
        ).reshape(seq_length, model_width)
        * score_scale
    )
    value_part = jnp.einsum(
        "hqk,qhd->khd",
        probs_again.astype(jnp.bfloat16),
        attended_heads,
        preferred_element_type=jnp.float32,
    ).reshape(seq_length, model_width)
    key_grad, value_grad = (
        lax.psum_scatter(
            key_part.astype(jnp.bfloat16), "ctx", scatter_dimension=0, tiled=True
        ).astype(jnp.float32),
        lax.psum_scatter(
            value_part.astype(jnp.bfloat16), "ctx", scatter_dimension=0, tiled=True
        ).astype(jnp.float32),
    )
    query_value, query_back = jax.vjp(norm_rope, query_pre, gain_table[:, 1])
    query_pre_grad, gain_query_grad = query_back(query_grad)
    key_value, key_back = jax.vjp(norm_rope, key_pre, gain_table[:, 2])
    key_pre_grad, gain_key_grad = key_back(key_grad)
    query_low = query_pre_grad.astype(jnp.bfloat16)
    key_low = key_pre_grad.astype(jnp.bfloat16)
    value_low = value_grad.astype(jnp.bfloat16)
    first_grad = jnp.einsum("tf,df->td", query_low, query_full, preferred_element_type=jnp.float32)
    first_grad = first_grad + jnp.einsum(
        "tf,df->td", key_low, key_full, preferred_element_type=jnp.float32
    )
    first_grad = first_grad + jnp.einsum(
        "tf,df->td", value_low, value_full, preferred_element_type=jnp.float32
    )
    first_value, first_back = jax.vjp(rms_scale, tokens, gain_table[:, 0])
    token_part, gain_one_grad = first_back(first_grad)
    input_grad = (hidden_grad + token_part)[None]
    gain_grads = jnp.stack([gain_one_grad, gain_query_grad, gain_key_grad, gain_two_grad], axis=1)
    query_w_grad = jnp.einsum(
        "td,tf->df", first_norm, query_low, preferred_element_type=jnp.float32
    )
    key_w_grad = jnp.einsum("td,tf->df", first_norm, key_low, preferred_element_type=jnp.float32)
    value_w_grad = jnp.einsum(
        "td,tf->df", first_norm, value_low, preferred_element_type=jnp.float32
    )
    output_w_grad = jnp.einsum(
        "td,tf->df", attended, hidden_grad_low, preferred_element_type=jnp.float32
    )
    router_grad = jnp.einsum(
        "td,te->de", second_norm, logit_grad, preferred_element_type=jnp.float32
    )
    query_share, key_share, value_share, output_share, router_share, gain_share = (
        lax.psum_scatter(
            query_w_grad.astype(jnp.bfloat16), "exp", scatter_dimension=0, tiled=True
        ).astype(jnp.float32),
        lax.psum_scatter(
            key_w_grad.astype(jnp.bfloat16), "exp", scatter_dimension=0, tiled=True
        ).astype(jnp.float32),
        lax.psum_scatter(
            value_w_grad.astype(jnp.bfloat16), "exp", scatter_dimension=0, tiled=True
        ).astype(jnp.float32),
        lax.psum_scatter(
            output_w_grad.astype(jnp.bfloat16), "exp", scatter_dimension=0, tiled=True
        ).astype(jnp.float32),
        lax.psum_scatter(
            router_grad.astype(jnp.bfloat16), "exp", scatter_dimension=0, tiled=True
        ).astype(jnp.float32),
        lax.psum_scatter(
            gain_grads.astype(jnp.bfloat16), "exp", scatter_dimension=0, tiled=True
        ).astype(jnp.float32),
    )
    query_sum, key_sum, value_sum, output_sum, router_sum, gain_sum = (
        lax.psum(query_share.astype(jnp.bfloat16), "ctx").astype(jnp.float32),
        lax.psum(key_share.astype(jnp.bfloat16), "ctx").astype(jnp.float32),
        lax.psum(value_share.astype(jnp.bfloat16), "ctx").astype(jnp.float32),
        lax.psum(output_share.astype(jnp.bfloat16), "ctx").astype(jnp.float32),
        lax.psum(router_share.astype(jnp.bfloat16), "ctx").astype(jnp.float32),
        lax.psum(gain_share.astype(jnp.bfloat16), "ctx").astype(jnp.float32),
    )
    return (
        output,
        input_grad,
        query_sum,
        key_sum,
        value_sum,
        output_sum,
        router_sum,
        gain_sum,
        gate_up_grad,
        down_grad_shard,
    )


def solution(mesh):
    in_specs = (
        P("exp", "ctx", None),
        P("exp", None),
        P("exp", "ctx", None),
        P("exp", None),
        P("exp", None),
        P("exp", None),
        P("exp", None),
        P("exp", None),
        P("exp", None),
        P("exp", None, "ctx"),
        P("exp", None, "ctx"),
        P("exp", "ctx", None),
    )
    out_specs = (
        P("exp", "ctx", None),
        P("exp", "ctx", None),
        P("exp", None),
        P("exp", None),
        P("exp", None),
        P("exp", None),
        P("exp", None),
        P("exp", None),
        P("exp", None, "ctx"),
        P("exp", None, "ctx"),
    )
    return jax.shard_map(
        per_device, mesh=mesh, in_specs=in_specs, out_specs=out_specs, check_vma=False
    )
```

profile of v0, /device:TPU:0, one launch (start us, length us, event | category | flops | bytes accessed | tf_op | source)
XLA Modules:
  0.0 3466.2 jit_solution(3763846171016239692)
XLA Ops:
  12.2 28.3 all_gather.32
  42.1 96.0 %all-gather.13.cloned.1.call-done = bf16[2048,2048]{1,0:T(8,128)(2,1)} async-done(((bf16[256,2048]{1,0:T(8,128)(2,1)}), bf16[2048,2048]{1,0:T(8,128)(2,1)}) %all-gather.13.cloned.1.call-update) | async-done | bytes 8388624 | tf_op jit(solution)/shard_map/all_gather | solution.py:65
  147.7 115.6 %all-gather.15.cloned.1.call-done = bf16[2048,2048]{1,0:T(8,128)(2,1)} async-done(((bf16[256,2048]{1,0:T(8,128)(2,1)}), bf16[2048,2048]{1,0:T(8,128)(2,1)}) %all-gather.15.cloned.1.call-update) | async-done | bytes 8388624 | tf_op jit(solution)/shard_map/all_gather | solution.py:66
  272.8 11.4 slice_negate_fusion.1
  297.9 90.8 %all-gather.9.cloned.1.call-done = bf16[2048,2048]{1,0:T(8,128)(2,1)} async-done(((bf16[256,2048]{1,0:T(8,128)(2,1)}), bf16[2048,2048]{1,0:T(8,128)(2,1)}) %all-gather.9.cloned.1.call-update) | async-done | bytes 8388624 | tf_op jit(solution)/shard_map/all_gather | solution.py:67
  388.6 8.5 convolution_convert_fusion.10
  403.7 30.5 all_gather.39
  438.8 9.3 copy.158
  448.1 17.8 fusion
  466.0 17.2 exponential_reduce_fusion
  483.6 20.2 fusion.44
  503.9 106.7 %all-gather.19.cloned.1.call-done = bf16[2048,2048]{1,0:T(8,128)(2,1)} async-done(((bf16[256,2048]{1,0:T(8,128)(2,1)}), bf16[2048,2048]{1,0:T(8,128)(2,1)}) %all-gather.19.cloned.1.call-update) | async-done | bytes 8388624 | tf_op jit(solution)/shard_map/all_gather | solution.py:68
  620.7 27.9 scatter_custom_fusion.1
  648.7 13.5 slice.79
  669.2 26.6 scatter_custom_fusion
  695.8 13.6 slice.76
  709.4 298.7 %all-to-all-done.2 = bf16[16,240,2048]{2,1,0:T(8,128)(2,1)} async-done(((bf16[16,240,2048]{2,1,0:T(8,128)(2,1)}), bf16[16,240,2048]{2,1,0:T(8,128)(2,1)}, u32[]{:S(2)}, u32[]{:S(2)}) %all-to-all-start.2) | async-done | bytes 15728672 | tf_op jit(solution)/shard_map/all_to_all | solution.py:168
  1014.4 14.3 copy.132
  1028.7 324.3 %all-to-all-done = bf16[16,240,2048]{2,1,0:T(8,128)(2,1)} async-done(((bf16[16,240,2048]{2,1,0:T(8,128)(2,1)}), bf16[16,240,2048]{2,1,0:T(8,128)(2,1)}, u32[]{:S(2)}, u32[]{:S(2)}) %all-to-all-start) | async-done | bytes 15728672 | tf_op jit(solution)/shard_map/all_to_all | solution.py:138
  1353.0 13.5 copy.128
  1366.5 23.6 fusion.15
  1390.2 21.1 fusion.19
  1411.3 32.9 multiply_convert_fusion.1
  1444.1 23.5 convolution_convert_fusion
  1467.7 29.1 copy.129
  1502.4 25.0 fusion.17
  1527.5 26.5 add_convert_fusion
  1553.9 29.1 copy.133
  1583.1 258.1 %all-to-all-done.1 = bf16[2,1920,2048]{2,0,1:T(2,128)(2,1)} async-done(((bf16[2,1920,2048]{2,0,1:T(2,128)(2,1)}), bf16[2,1920,2048]{2,0,1:T(2,128)(2,1)}, u32[]{:S(2)}, u32[]{:S(2)}) %all-to-all-start.1) | async-done | bytes 15728672 | tf_op jit(solution)/shard_map/all_to_all | solution.py:152
  1846.9 11.8 copy.130
  1858.8 7.1 concatenate.30
  1865.9 31.5 gather_fusion
  1897.4 13.1 fusion.2
  1912.2 274.1 %all-to-all-done.3 = bf16[2,1920,2048]{2,0,1:T(2,128)(2,1)} async-done(((bf16[2,1920,2048]{2,0,1:T(2,128)(2,1)}), bf16[2,1920,2048]{2,0,1:T(2,128)(2,1)}, u32[]{:S(2)}, u32[]{:S(2)}) %all-to-all-start.3) | async-done | bytes 15728672 | tf_op jit(solution)/shard_map/all_to_all | solution.py:204
  2186.4 11.6 copy.134
  2198.0 7.1 concatenate.31
  2205.2 31.3 gather_fusion.1
  2236.5 11.1 convert_reduce_fusion
  2260.4 18.4 convolution_convert_fusion.8
  2278.8 8.6 copy.153
  2287.5 31.7 multiply_reduce_fusion
  2319.2 32.1 multiply_convert_fusion
  2351.4 12.5 multiply_convert_fusion.4
  2363.8 8.8 copy.151
  2374.5 8.7 convolution_convert_fusion.1
  2384.1 13.5 bitcast_multiply_fusion.5
  2419.0 8.4 convolution_convert_fusion.2
  2443.1 7.0 convolution_convert_fusion.3
  2450.1 24.0 convolution_convert_fusion.5
  2474.3 23.0 convolution_convert_fusion.6
  2497.3 22.7 convolution_convert_fusion.7
  2520.0 7.5 pad_maximum_fusion
  2535.2 8.8 fusion.81
  2544.0 7.5 fusion.31
  2553.8 29.8 reduce-scatter.23.cloned.1.call-done
  2583.5 152.5 %reduce-scatter.17.cloned.1.call-done = bf16[256,2048]{1,0:T(8,128)(2,1)} async-done(((bf16[2048,2048]{1,0:T(8,128)(2,1)}), bf16[256,2048]{1,0:T(8,128)(2,1)}) %reduce-scatter.17.cloned.1.call-update) | async-done | bytes 1048592 | tf_op jit(solution)/shard_map/reduce_scatter | solution.py:292
  2736.0 151.7 %reduce-scatter.21.cloned.1.call-done = bf16[256,2048]{1,0:T(8,128)(2,1)} async-done(((bf16[2048,2048]{1,0:T(8,128)(2,1)}), bf16[256,2048]{1,0:T(8,128)(2,1)}) %reduce-scatter.21.cloned.1.call-update) | async-done | bytes 1048592 | tf_op jit(solution)/shard_map/reduce_scatter | solution.py:298
  2887.7 152.0 %reduce-scatter.19.cloned.1.call-done = bf16[256,2048]{1,0:T(8,128)(2,1)} async-done(((bf16[2048,2048]{1,0:T(8,128)(2,1)}), bf16[256,2048]{1,0:T(8,128)(2,1)}) %reduce-scatter.19.cloned.1.call-update) | async-done | bytes 1048592 | tf_op jit(solution)/shard_map/reduce_scatter | solution.py:295
  3039.7 73.1 %reduce-scatter.29.cloned.1.call-done = bf16[2,2048,256]{2,1,0:T(8,128)(2,1)} async-done(((bf16[2,2048,1024]{2,1,0:T(8,128)(2,1)}), bf16[2,2048,256]{2,1,0:T(8,128)(2,1)}) %reduce-scatter.29.cloned.1.call-update) | async-done | bytes 2097168 | tf_op jit(solution)/shard_map/reduce_scatter | solution.py:200
  3116.8 124.8 %reduce-scatter.27.cloned.1.call-done = bf16[2,4096,256]{2,1,0:T(8,128)(2,1)} async-done(((bf16[2,4096,1024]{2,1,0:T(8,128)(2,1)}), bf16[2,4096,256]{2,1,0:T(8,128)(2,1)}) %reduce-scatter.27.cloned.1.call-update) | async-done | bytes 4194320 | tf_op jit(solution)/shard_map/reduce_scatter | solution.py:194
  3250.6 56.8 %reduce-scatter.35.cloned.1.call-done = bf16[256,4]{1,0:T(8,128)(2,1)} async-done(((bf16[2048,4]{1,0:T(8,128)(2,1)}), bf16[256,4]{1,0:T(8,128)(2,1)}) %reduce-scatter.35.cloned.1.call-update) | async-done | bytes 2064
  3308.3 55.6 %reduce-scatter.25.cloned.1.call-done = bf16[256,16]{0,1:T(8,128)(2,1)} async-done(((bf16[2048,16]{0,1:T(8,128)(2,1)}), bf16[256,16]{0,1:T(8,128)(2,1)}) %reduce-scatter.25.cloned.1.call-update) | async-done | bytes 8208 | tf_op jit(solution)/shard_map/reduce_scatter | solution.py:304
  3363.9 10.1 all-reduce.6
  3375.3 76.6 %all-reduce.10.cloned.1.call-done = (bf16[256,2048]{1,0:T(8,128)(2,1)}, bf16[256,2048]{1,0:T(8,128)(2,1)}, bf16[256,2048]{1,0:T(8,128)(2,1)}, bf16[256,2048]{1,0:T(8,128)(2,1)}) async-done(((bf16[256,2048]{1,0:T(8,128)(2,1)}, bf16[256,2048]{1,0:T(8,128)(2,1)}, bf16[256,2048]{1,0:T(8,128)(2,1)}, bf16[256,2048]{1,0:T(8,128)(2,1)}), (bf16[256,2048]{1,0:T(8,128)(2,1)}, bf16[256,2048]{1,0:T(8,128)(2,1)}, ...) | async-done | bytes 4194320 | tf_op jit(solution)/shard_map/psum | solution.py:312
  (343 shorter events, 172.0 us)
Async XLA Ops:
  7.2 33.3 copy-start.18
  7.2 130.9 %all-gather.13.cloned.1.call-start = ((), (), s32[]{:S(2)}) async-start(), calls=%async_computation.16 | async-start | bytes 9437184 | tf_op jit(solution)/shard_map/all_gather | solution.py:65
  7.9 255.4 %all-gather.15.cloned.1.call-start = ((), (), s32[]{:S(2)}) async-start(), calls=%async_computation.17 | async-start | bytes 9437184 | tf_op jit(solution)/shard_map/all_gather | solution.py:66
  8.7 379.9 %all-gather.9.cloned.1.call-start = ((), (), s32[]{:S(2)}) async-start(), calls=%async_computation.14 | async-start | bytes 9437184 | tf_op jit(solution)/shard_map/all_gather | solution.py:67
  9.4 429.4 %all-gather.17.cloned.1.call-start = ((), (), s32[]{:S(2)}) async-start(), calls=%async_computation.18 | async-start | bytes 7864320 | tf_op jit(solution)/shard_map/all_gather | solution.py:96
  12.0 272.3 %copy-start.31 = (f32[384,128]{1,0:T(8,128)}, f32[384,128]{1,0:T(8,128)S(1)}, u32[]{:S(2)}) copy-start(f32[384,128]{1,0:T(8,128)S(1)} %copy.120) | copy-start | bytes 589828
  12.1 278.5 %copy-start.35 = (f32[384,128]{1,0:T(8,128)}, f32[384,128]{1,0:T(8,128)S(1)}, u32[]{:S(2)}) copy-start(f32[384,128]{1,0:T(8,128)S(1)} %copy.119) | copy-start | bytes 589828
  40.8 97.2 %copy-start.78 = (f32[384]{0:T(512)}, f32[384]{0:T(512)S(1)}, u32[]{:S(2)}) copy-start(f32[384]{0:T(512)S(1)} %fusion.37) | copy-start | bytes 4612
  42.0 248.8 %copy-start.50 = (f32[2048,1]{0,1:T(1,128)}, f32[2048,1]{0,1:T(1,128)S(1)}, u32[]{:S(2)}) copy-start(f32[2048,1]{0,1:T(1,128)S(1)} %get-tuple-element.50) | copy-start | bytes 24580
  42.1 248.9 %copy-start.52 = (f32[2048,1]{0,1:T(1,128)}, f32[2048,1]{0,1:T(1,128)S(1)}, u32[]{:S(2)}) copy-start(f32[2048,1]{0,1:T(1,128)S(1)} %get-tuple-element.51) | copy-start | bytes 24580
  144.6 146.3 %copy-start.2 = (f32[384,2048]{1,0:T(8,128)}, f32[384,2048]{1,0:T(8,128)S(1)}, u32[]{:S(2)}) copy-start(f32[384,2048]{1,0:T(8,128)S(1)} %get-tuple-element.56) | copy-start | bytes 9437188
  269.9 21.0 copy-start
  270.0 21.0 copy-start.64
  291.4 97.3 %copy-start.76 = (f32[2048,1]{0,1:T(1,128)S(1)}, f32[2048,1]{0,1:T(1,128)}, u32[]{:S(2)}) copy-start(f32[2048,1]{0,1:T(1,128)} %get-tuple-element.52) | copy-start | bytes 24580
  291.4 97.3 %copy-start.84 = (f32[384]{0:T(512)S(1)}, f32[384]{0:T(512)}, u32[]{:S(2)}) copy-start(f32[384]{0:T(512)} %fusion.59) | copy-start | bytes 4612
  297.6 100.1 %copy-start.54 = (s32[1,384,8]{1,2,0:T(8,128)S(1)}, s32[1,384,8]{1,2,0:T(8,128)}, u32[]{:S(2)}) copy-start(s32[1,384,8]{1,2,0:T(8,128)} %param.14) | copy-start | bytes 36868
  297.6 186.0 %all-gather.11.cloned.1.call-start = ((), (), s32[]{:S(2)}) async-start(), calls=%async_computation.15 | async-start | bytes 7864320 | tf_op jit(solution)/shard_map/all_gather | solution.py:97
  397.1 37.3 %copy-start.72 = (s32[1536]{0:T(1024)S(1)}, s32[1536]{0:T(1024)}, u32[]{:S(2)}) copy-start(s32[1536]{0:T(1024)} %copy-done.71) | copy-start | bytes 18436
  397.1 37.3 %copy-start.86 = (s32[384]{0:T(512)S(1)}, s32[384]{0:T(512)}, u32[]{:S(2)}) copy-start(s32[384]{0:T(512)} %get-tuple-element.27) | copy-start | bytes 4612
  397.1 37.7 %copy-start.27 = (bf16[1,384,2048]{2,1,0:T(8,128)(2,1)S(1)}, bf16[1,384,2048]{2,1,0:T(8,128)(2,1)}, u32[]{:S(2)}) copy-start(bf16[1,384,2048]{2,1,0:T(8,128)(2,1)} %param.23) | copy-start | bytes 4718596
  397.1 213.4 %all-gather.19.cloned.1.call-start = ((), (), s32[]{:S(2)}) async-start(), calls=%async_computation.19 | async-start | bytes 9437184 | tf_op jit(solution)/shard_map/all_gather | solution.py:68
  434.2 183.3 %copy-start.48 = (bf16[2048,16]{0,1:T(8,128)(2,1)}, bf16[2048,16]{0,1:T(8,128)(2,1)S(1)}, u32[]{:S(2)}) copy-start(bf16[2048,16]{0,1:T(8,128)(2,1)S(1)} %all_gather.39) | copy-start | bytes 196612
  434.8 48.8 %copy-start.6 = (pred[384,1536]{1,0:T(8,128)(4,1)}, pred[384,1536]{1,0:T(8,128)(4,1)S(1)}, u32[]{:S(2)}) copy-start(pred[384,1536]{1,0:T(8,128)(4,1)S(1)} %broadcast_compare_fusion) | copy-start | bytes 1769476
  436.9 231.7 %copy-start.69 = (s32[3072,1]{0,1:T(1,128)}, s32[3072,1]{0,1:T(1,128)S(1)}, u32[]{:S(2)}) copy-start(s32[3072,1]{0,1:T(1,128)S(1)} %compare_select_fusion) | copy-start | bytes 36868
  438.8 9.3 copy-start.11
  483.2 20.7 copy-start.45
  483.2 127.4 %copy-start.19 = (bf16[1,384,2048]{2,1,0:T(8,128)(2,1)S(1)}, bf16[1,384,2048]{2,1,0:T(8,128)(2,1)}, u32[]{:S(2)}) copy-start(bf16[1,384,2048]{2,1,0:T(8,128)(2,1)} %param.12) | copy-start | bytes 4718596
  620.3 28.4 copy-start.33
  662.1 345.9 %all-to-all-start.2 = ((bf16[16,240,2048]{2,1,0:T(8,128)(2,1)}), bf16[16,240,2048]{2,1,0:T(8,128)(2,1)}, u32[]{:S(2)}, u32[]{:S(2)}) async-start(bf16[16,240,2048]{2,1,0:T(8,128)(2,1)} %bitcast.209), calls=%async_computation.2 | async-start | bytes 31457280 | tf_op jit(solution)/shard_map/all_to_all | solution.py:168
  667.8 698.7 %all-gather.21.cloned.1.call-start = ((), (), s32[]{:S(2)}) async-start(), calls=%async_computation.20 | async-start | bytes 20971520 | tf_op jit(solution)/shard_map/all_gather | solution.py:140
  1008.0 345.0 %all-to-all-start = ((bf16[16,240,2048]{2,1,0:T(8,128)(2,1)}), bf16[16,240,2048]{2,1,0:T(8,128)(2,1)}, u32[]{:S(2)}, u32[]{:S(2)}) async-start(bf16[16,240,2048]{2,1,0:T(8,128)(2,1)} %bitcast.208), calls=%async_computation | async-start | bytes 31457280 | tf_op jit(solution)/shard_map/all_to_all | solution.py:138
  1013.7 397.6 %all-gather.23.cloned.1.call-start = ((), (), s32[]{:S(2)}) async-start(), calls=%async_computation.21 | async-start | bytes 10485760 | tf_op jit(solution)/shard_map/all_gather | solution.py:141
  1366.5 23.6 copy-start.17
  1496.8 344.4 %all-to-all-start.1 = ((bf16[2,1920,2048]{2,0,1:T(2,128)(2,1)}), bf16[2,1920,2048]{2,0,1:T(2,128)(2,1)}, u32[]{:S(2)}, u32[]{:S(2)}) async-start(bf16[2,1920,2048]{2,0,1:T(2,128)(2,1)} %copy.129), calls=%async_computation.1 | async-start | bytes 31457280 | tf_op jit(solution)/shard_map/all_to_all | solution.py:152
  1583.1 263.9 %copy-start.70 = (s32[3072,1]{0,1:T(1,128)S(1)}, s32[3072,1]{0,1:T(1,128)}, u32[]{:S(2)}) copy-start(s32[3072,1]{0,1:T(1,128)} %copy-done.69) | copy-start | bytes 36868
  1841.2 345.2 %all-to-all-start.3 = ((bf16[2,1920,2048]{2,0,1:T(2,128)(2,1)}), bf16[2,1920,2048]{2,0,1:T(2,128)(2,1)}, u32[]{:S(2)}, u32[]{:S(2)}) async-start(bf16[2,1920,2048]{2,0,1:T(2,128)(2,1)} %copy.133), calls=%async_computation.3 | async-start | bytes 31457280 | tf_op jit(solution)/shard_map/all_to_all | solution.py:204
  1846.9 570.9 %reduce-scatter.33.cloned.1.call-start = ((), (), s32[]{:S(2)}) async-start(), calls=%async_computation.30 | async-start | bytes 7864320
  1846.9 19.0 copy-start.58
  1865.9 31.5 copy-start.10
  1865.9 31.5 copy-start.34
  1897.4 13.2 copy-start.55
  1897.4 13.3 copy-start.63
  1912.2 335.4 %copy-start.60 = (bf16[384,16]{0,1:T(8,128)(2,1)}, bf16[384,16]{0,1:T(8,128)(2,1)S(1)}, u32[]{:S(2)}) copy-start(bf16[384,16]{0,1:T(8,128)(2,1)S(1)} %multiply_convert_fusion.6) | copy-start | bytes 36868
  2236.5 11.1 copy-start.5
  2236.5 11.1 copy-start.49
  2236.5 11.1 copy-start.57
  2236.5 11.1 copy-start.74
  2287.4 143.5 %reduce-scatter.31.cloned.1.call-start = ((), (), s32[]{:S(2)}) async-start(), calls=%async_computation.29 | async-start | bytes 7864320
  2319.2 32.1 copy-start.12
  2372.6 210.9 %reduce-scatter.23.cloned.1.call-start = ((), (), s32[]{:S(2)}) async-start(), calls=%async_computation.25 | async-start | bytes 9437184 | tf_op jit(solution)/shard_map/reduce_scatter | solution.py:301
  2383.2 352.9 %reduce-scatter.17.cloned.1.call-start = ((), (), s32[]{:S(2)}) async-start(), calls=%async_computation.22 | async-start | bytes 9437184 | tf_op jit(solution)/shard_map/reduce_scatter | solution.py:292
  2417.6 470.1 %reduce-scatter.21.cloned.1.call-start = ((), (), s32[]{:S(2)}) async-start(), calls=%async_computation.24 | async-start | bytes 9437184 | tf_op jit(solution)/shard_map/reduce_scatter | solution.py:298
  2427.4 612.3 %reduce-scatter.19.cloned.1.call-start = ((), (), s32[]{:S(2)}) async-start(), calls=%async_computation.23 | async-start | bytes 9437184 | tf_op jit(solution)/shard_map/reduce_scatter | solution.py:295
  2450.1 662.8 %reduce-scatter.29.cloned.1.call-start = ((), (), s32[]{:S(2)}) async-start(), calls=%async_computation.28 | async-start | bytes 10485760 | tf_op jit(solution)/shard_map/reduce_scatter | solution.py:200
  2474.2 767.4 %reduce-scatter.27.cloned.1.call-start = ((), (), s32[]{:S(2)}) async-start(), calls=%async_computation.27 | async-start | bytes 20971520 | tf_op jit(solution)/shard_map/reduce_scatter | solution.py:194
  2527.5 779.8 %reduce-scatter.35.cloned.1.call-start = ((), (), s32[]{:S(2)}) async-start(), calls=%async_computation.31 | async-start | bytes 589824
  2529.0 15.0 slice-start.2
  2535.2 8.8 slice-start.3
  2535.2 8.8 copy-start.93
  2544.0 8.7 copy-start.15
  2544.0 8.7 copy-start.61
  2552.7 811.3 %reduce-scatter.25.cloned.1.call-start = ((), (), s32[]{:S(2)}) async-start(), calls=%async_computation.26 | async-start | bytes 73728 | tf_op jit(solution)/shard_map/reduce_scatter | solution.py:304
  2553.7 898.1 %all-reduce.10.cloned.1.call-start = ((), (), s32[]{:S(2)}) async-start(), calls=%async_computation.32 | async-start | bytes 8388608 | tf_op jit(solution)/shard_map/psum | solution.py:312
  3116.8 131.2 %copy-start.79 = (f32[384]{0:T(512)S(1)}, f32[384]{0:T(512)}, u32[]{:S(2)}) copy-start(f32[384]{0:T(512)} %copy-done.78) | copy-start | bytes 4612
  (58 other events, 146.6 us)
Sparse Core Ops, SparseCore 0:
  10.2 127.8 all-gather.12
  140.2 123.1 all-gather.14
  265.5 123.1 all-gather.8
  390.6 44.5 all-gather.16
  437.2 46.3 all-gather.10
  485.6 124.9 all-gather.18
  670.2 109.4 all-gather.20
  1016.1 60.6 all-gather.22
  2287.6 58.2 reduce-scatter.32
  2372.7 58.1 reduce-scatter.30
  2434.5 148.9 reduce-scatter.22
  2588.0 147.9 reduce-scatter.16
  2739.7 148.0 reduce-scatter.20
  2891.7 147.9 reduce-scatter.18
  3042.1 70.7 reduce-scatter.28
  3115.5 126.0 reduce-scatter.26
  3245.4 61.9 reduce-scatter.34
  3311.3 52.6 reduce-scatter.24
  3366.7 85.1 all-reduce.9
where the time goes:
time: 3480 us; the launch traced here: 3470 us
  waiting for transfers between devices  2450 us (70%)
  matrix products  426 us (12%)
  local copies, waits for them, and re-layouts  305 us (9%)
  other arithmetic  182 us (5%)
  blocking collectives  69 us (2%)
    all_to_all x1, waiting for transfers between devices, per_device(): lax.all_to_all(send_rows, 'exp', split_axis=0, concat_axis=1, tiled=True)  324 us
    all_to_all x1, waiting for transfers between devices, per_device(): lax.all_to_all(send_grad, 'exp', split_axis=0, concat_axis=1, tiled=True)  299 us
    all_to_all x1, waiting for transfers between devices, per_device(): lax.all_to_all(arrived_grad, 'exp', split_axis=1, concat_axis=0, tiled=True)  274 us
    all_to_all x1, waiting for transfers between devices, per_device(): lax.all_to_all(expert_out, 'exp', split_axis=1, concat_axis=0, tiled=True)  258 us
    reduce_scatter x1, waiting for transfers between devices, per_device(): lax.psum_scatter(query_w_grad.astype(jnp.bfloat16), 'exp', scatter_dimens...  153 us
    reduce_scatter x1, waiting for transfers between devices, per_device(): lax.psum_scatter(key_w_grad.astype(jnp.bfloat16), 'exp', scatter_dimensio...  152 us
    reduce_scatter x1, waiting for transfers between devices, per_device(): lax.psum_scatter(value_w_grad.astype(jnp.bfloat16), 'exp', scatter_dimens...  152 us
    reduce_scatter x1, waiting for transfers between devices, per_device(): lax.psum_scatter(jnp.concatenate([gate_w_grad, up_w_grad], axis=1).astype...  125 us
  transfers between devices with their start and end apart: 23, of which 19 were waited for; matrix products, arithmetic and copies ran while one was open for 19% of the time, Pallas kernels for 0%

commit v1 on v0

--- a/solution.py
+++ b/solution.py
@@ -6,6 +6,18 @@
 HEAD_DIM = 128
 epsilon = 1e-05
 rope_theta = 10000.0
+
+
+def ring_gather(value, axis, dim):
+    ways, here, lap = (lax.axis_size(axis), lax.axis_index(axis), value.shape[dim])
+    shape = [n * ways if d == dim else n for d, n in enumerate(value.shape)]
+    full = lax.dynamic_update_slice_in_dim(
+        jnp.zeros(shape, value.dtype), value, here * lap, axis=dim
+    )
+    for far in range(1, ways):
+        value = lax.ppermute(value, axis, [(d, (d + 1) % ways) for d in range(ways)])
+        full = lax.dynamic_update_slice_in_dim(full, value, (here - far) % ways * lap, axis=dim)
+    return full
 
 
 def rms_scale(matrix, gain):
@@ -64,7 +76,7 @@
     query_full, key_full, value_full, output_full, router_full, gains_bf = (
         lax.all_gather(w_query, "exp", axis=0, tiled=True),
         lax.all_gather(w_key, "exp", axis=0, tiled=True),
-        lax.all_gather(w_value, "exp", axis=0, tiled=True),
+        ring_gather(w_value, "exp", 0),
         lax.all_gather(w_output, "exp", axis=0, tiled=True),
         lax.all_gather(w_router, "exp", axis=0, tiled=True),
         lax.all_gather(norm_gains, "exp", axis=0, tiled=True),

time: 3480 us -> 3520 us (1.011)
    ppermute x0 -> x7, waiting for transfers between devices: none -> 167 us  [ring_gather(): lax.ppermute(value, axis, [(d, (d + 1) % ways) for d in range(ways)])]
    all_gather x1 -> x0, waiting for transfers between devices: 90.8 us -> none  [per_device(): lax.all_gather(w_value, 'exp', axis=0, tiled=True)]
    all_gather x1, waiting for transfers between devices: 107 us -> 64.5 us  [per_device(): lax.all_gather(w_output, 'exp', axis=0, tiled=True)]
  transfers between devices with their start and end apart: 23 -> 29, of which waited for: 19 -> 24; matrix products, arithmetic and copies ran while one was open for 19% -> 18% of each run, Pallas kernels for 0% -> 0%
where the time goes in v1:
time: 3520 us; the launch traced here: 3510 us
  waiting for transfers between devices  2480 us (70%)
  matrix products  425 us (12%)
  local copies, waits for them, and re-layouts  314 us (9%)
  other arithmetic  182 us (5%)
  blocking collectives  69 us (2%)
    all_to_all x1, waiting for transfers between devices, per_device(): lax.all_to_all(send_rows, 'exp', split_axis=0, concat_axis=1, tiled=True)  324 us
    all_to_all x1, waiting for transfers between devices, per_device(): lax.all_to_all(send_grad, 'exp', split_axis=0, concat_axis=1, tiled=True)  299 us
    all_to_all x1, waiting for transfers between devices, per_device(): lax.all_to_all(arrived_grad, 'exp', split_axis=1, concat_axis=0, tiled=True)  274 us
    all_to_all x1, waiting for transfers between devices, per_device(): lax.all_to_all(expert_out, 'exp', split_axis=1, concat_axis=0, tiled=True)  258 us
    ppermute x7, waiting for transfers between devices, ring_gather(): lax.ppermute(value, axis, [(d, (d + 1) % ways) for d in range(ways)])  167 us
    reduce_scatter x1, waiting for transfers between devices, per_device(): lax.psum_scatter(query_w_grad.astype(jnp.bfloat16), 'exp', scatter_dimens...  152 us
    reduce_scatter x1, waiting for transfers between devices, per_device(): lax.psum_scatter(key_w_grad.astype(jnp.bfloat16), 'exp', scatter_dimensio...  152 us
    reduce_scatter x1, waiting for transfers between devices, per_device(): lax.psum_scatter(value_w_grad.astype(jnp.bfloat16), 'exp', scatter_dimens...  152 us
  transfers between devices with their start and end apart: 29, of which 24 were waited for; matrix products, arithmetic and copies ran while one was open for 18% of the time, Pallas kernels for 0%

profile of v1, /device:TPU:0, one launch (start us, length us, event | category | flops | bytes accessed | tf_op | source)
XLA Modules:
  0.0 3505.2 jit_solution(7036273836250790285)
XLA Ops:
  12.1 28.3 all_gather.29
  42.0 96.0 %all-gather.10.cloned.1.call-done = bf16[2048,2048]{1,0:T(8,128)(2,1)} async-done(((bf16[256,2048]{1,0:T(8,128)(2,1)}), bf16[2048,2048]{1,0:T(8,128)(2,1)}) %all-gather.10.cloned.1.call-update) | async-done | bytes 8388624 | tf_op jit(solution)/shard_map/all_gather | solution.py:77
  147.7 115.6 %all-gather.12.cloned.1.call-done = bf16[2048,2048]{1,0:T(8,128)(2,1)} async-done(((bf16[256,2048]{1,0:T(8,128)(2,1)}), bf16[2048,2048]{1,0:T(8,128)(2,1)}) %all-gather.12.cloned.1.call-update) | async-done | bytes 8388624 | tf_op jit(solution)/shard_map/all_gather | solution.py:78
  272.7 11.1 slice_negate_fusion.1
  297.9 26.8 collective-permute-done
  324.8 26.3 collective-permute-done.1
  351.1 25.3 collective-permute-done.2
  376.4 24.4 collective-permute-done.3
  401.8 23.6 collective-permute-done.4
  426.9 21.8 collective-permute-done.5
  451.9 18.8 collective-permute-done.6
  485.4 30.5 all_gather.35
  520.6 9.2 copy.158
  529.8 18.1 fusion
  547.9 17.2 exponential_reduce_fusion
  565.1 20.0 fusion.44
  585.1 64.5 %all-gather.16.cloned.1.call-done = bf16[2048,2048]{1,0:T(8,128)(2,1)} async-done(((bf16[256,2048]{1,0:T(8,128)(2,1)}), bf16[2048,2048]{1,0:T(8,128)(2,1)}) %all-gather.16.cloned.1.call-update) | async-done | bytes 8388624 | tf_op jit(solution)/shard_map/all_gather | solution.py:80
  659.8 28.0 scatter_custom_fusion.1
  687.8 13.5 slice.79
  708.3 26.6 scatter_custom_fusion
  734.8 13.6 slice.76
  748.4 298.7 %all-to-all-done.2 = bf16[16,240,2048]{2,1,0:T(8,128)(2,1)} async-done(((bf16[16,240,2048]{2,1,0:T(8,128)(2,1)}), bf16[16,240,2048]{2,1,0:T(8,128)(2,1)}, u32[]{:S(2)}, u32[]{:S(2)}) %all-to-all-start.2) | async-done | bytes 15728672 | tf_op jit(solution)/shard_map/all_to_all | solution.py:180
  1053.5 14.3 copy.132
  1067.8 324.3 %all-to-all-done = bf16[16,240,2048]{2,1,0:T(8,128)(2,1)} async-done(((bf16[16,240,2048]{2,1,0:T(8,128)(2,1)}), bf16[16,240,2048]{2,1,0:T(8,128)(2,1)}, u32[]{:S(2)}, u32[]{:S(2)}) %all-to-all-start) | async-done | bytes 15728672 | tf_op jit(solution)/shard_map/all_to_all | solution.py:150
  1392.1 13.5 copy.128
  1405.6 23.7 fusion.15
  1429.3 21.1 fusion.19
  1450.4 32.9 multiply_convert_fusion.1
  1483.2 23.5 convolution_convert_fusion
  1506.7 29.1 copy.129
  1541.5 25.0 fusion.17
  1566.5 26.4 add_convert_fusion
  1592.9 29.1 copy.133
  1622.1 258.2 %all-to-all-done.1 = bf16[2,1920,2048]{2,0,1:T(2,128)(2,1)} async-done(((bf16[2,1920,2048]{2,0,1:T(2,128)(2,1)}), bf16[2,1920,2048]{2,0,1:T(2,128)(2,1)}, u32[]{:S(2)}, u32[]{:S(2)}) %all-to-all-start.1) | async-done | bytes 15728672 | tf_op jit(solution)/shard_map/all_to_all | solution.py:164
  1886.0 11.8 copy.130
  1905.0 31.5 gather_fusion
  1936.5 13.1 fusion.2
  1951.3 274.1 %all-to-all-done.3 = bf16[2,1920,2048]{2,0,1:T(2,128)(2,1)} async-done(((bf16[2,1920,2048]{2,0,1:T(2,128)(2,1)}), bf16[2,1920,2048]{2,0,1:T(2,128)(2,1)}, u32[]{:S(2)}, u32[]{:S(2)}) %all-to-all-start.3) | async-done | bytes 15728672 | tf_op jit(solution)/shard_map/all_to_all | solution.py:216
  2225.4 11.6 copy.134
  2244.2 31.3 gather_fusion.1
  2275.6 11.1 convert_reduce_fusion
  2299.5 18.3 convolution_convert_fusion.8
  2317.8 8.7 copy.153
  2326.7 31.9 multiply_reduce_fusion
  2358.6 32.1 multiply_convert_fusion
  2390.7 12.5 multiply_convert_fusion.4
  2403.3 8.7 copy.151
  2413.9 8.7 convolution_convert_fusion.1
  2423.5 13.5 bitcast_multiply_fusion.5
  2489.4 24.1 convolution_convert_fusion.5
  2513.5 23.0 convolution_convert_fusion.6
  2536.6 22.7 convolution_convert_fusion.7
  2568.2 8.6 fusion.80
  2576.8 8.7 fusion.81
  2595.5 27.2 reduce-scatter.23.cloned.1.call-done
  2622.7 152.1 %reduce-scatter.17.cloned.1.call-done = bf16[256,2048]{1,0:T(8,128)(2,1)} async-done(((bf16[2048,2048]{1,0:T(8,128)(2,1)}), bf16[256,2048]{1,0:T(8,128)(2,1)}) %reduce-scatter.17.cloned.1.call-update) | async-done | bytes 1048592 | tf_op jit(solution)/shard_map/reduce_scatter | solution.py:304
  2774.9 151.5 %reduce-scatter.21.cloned.1.call-done = bf16[256,2048]{1,0:T(8,128)(2,1)} async-done(((bf16[2048,2048]{1,0:T(8,128)(2,1)}), bf16[256,2048]{1,0:T(8,128)(2,1)}) %reduce-scatter.21.cloned.1.call-update) | async-done | bytes 1048592 | tf_op jit(solution)/shard_map/reduce_scatter | solution.py:310
  2926.4 152.1 %reduce-scatter.19.cloned.1.call-done = bf16[256,2048]{1,0:T(8,128)(2,1)} async-done(((bf16[2048,2048]{1,0:T(8,128)(2,1)}), bf16[256,2048]{1,0:T(8,128)(2,1)}) %reduce-scatter.19.cloned.1.call-update) | async-done | bytes 1048592 | tf_op jit(solution)/shard_map/reduce_scatter | solution.py:307
  3078.5 73.2 %reduce-scatter.29.cloned.1.call-done = bf16[2,2048,256]{2,1,0:T(8,128)(2,1)} async-done(((bf16[2,2048,1024]{2,1,0:T(8,128)(2,1)}), bf16[2,2048,256]{2,1,0:T(8,128)(2,1)}) %reduce-scatter.29.cloned.1.call-update) | async-done | bytes 2097168 | tf_op jit(solution)/shard_map/reduce_scatter | solution.py:212
  3155.6 124.8 %reduce-scatter.27.cloned.1.call-done = bf16[2,4096,256]{2,1,0:T(8,128)(2,1)} async-done(((bf16[2,4096,1024]{2,1,0:T(8,128)(2,1)}), bf16[2,4096,256]{2,1,0:T(8,128)(2,1)}) %reduce-scatter.27.cloned.1.call-update) | async-done | bytes 4194320 | tf_op jit(solution)/shard_map/reduce_scatter | solution.py:206
  3289.4 56.8 %reduce-scatter.35.cloned.1.call-done = bf16[256,4]{1,0:T(8,128)(2,1)} async-done(((bf16[2048,4]{1,0:T(8,128)(2,1)}), bf16[256,4]{1,0:T(8,128)(2,1)}) %reduce-scatter.35.cloned.1.call-update) | async-done | bytes 2064
  3347.1 55.6 %reduce-scatter.25.cloned.1.call-done = bf16[256,16]{0,1:T(8,128)(2,1)} async-done(((bf16[2048,16]{0,1:T(8,128)(2,1)}), bf16[256,16]{0,1:T(8,128)(2,1)}) %reduce-scatter.25.cloned.1.call-update) | async-done | bytes 8208 | tf_op jit(solution)/shard_map/reduce_scatter | solution.py:316
  3402.7 10.2 all-reduce.6
  3414.1 76.4 %all-reduce.10.cloned.1.call-done = (bf16[256,2048]{1,0:T(8,128)(2,1)}, bf16[256,2048]{1,0:T(8,128)(2,1)}, bf16[256,2048]{1,0:T(8,128)(2,1)}, bf16[256,2048]{1,0:T(8,128)(2,1)}) async-done(((bf16[256,2048]{1,0:T(8,128)(2,1)}, bf16[256,2048]{1,0:T(8,128)(2,1)}, bf16[256,2048]{1,0:T(8,128)(2,1)}, bf16[256,2048]{1,0:T(8,128)(2,1)}), (bf16[256,2048]{1,0:T(8,128)(2,1)}, bf16[256,2048]{1,0:T(8,128)(2,1)}, ...) | async-done | bytes 4194320 | tf_op jit(solution)/shard_map/psum | solution.py:324
  (371 shorter events, 224.2 us)
Async XLA Ops:
  7.2 33.2 copy-start.18
  7.2 130.8 %all-gather.10.cloned.1.call-start = ((), (), s32[]{:S(2)}) async-start(), calls=%async_computation.15 | async-start | bytes 9437184 | tf_op jit(solution)/shard_map/all_gather | solution.py:77
  7.9 255.3 %all-gather.12.cloned.1.call-start = ((), (), s32[]{:S(2)}) async-start(), calls=%async_computation.16 | async-start | bytes 9437184 | tf_op jit(solution)/shard_map/all_gather | solution.py:78
  8.7 511.9 %all-gather.14.cloned.1.call-start = ((), (), s32[]{:S(2)}) async-start(), calls=%async_computation.17 | async-start | bytes 7864320 | tf_op jit(solution)/shard_map/all_gather | solution.py:108
  11.9 271.9 %copy-start.33 = (f32[384,128]{1,0:T(8,128)}, f32[384,128]{1,0:T(8,128)S(1)}, u32[]{:S(2)}) copy-start(f32[384,128]{1,0:T(8,128)S(1)} %copy.120) | copy-start | bytes 589828
  12.0 278.1 %copy-start.37 = (f32[384,128]{1,0:T(8,128)}, f32[384,128]{1,0:T(8,128)S(1)}, u32[]{:S(2)}) copy-start(f32[384,128]{1,0:T(8,128)S(1)} %copy.119) | copy-start | bytes 589828
  40.8 97.2 %copy-start.83 = (f32[384]{0:T(512)}, f32[384]{0:T(512)S(1)}, u32[]{:S(2)}) copy-start(f32[384]{0:T(512)S(1)} %fusion.37) | copy-start | bytes 4612
  42.0 248.4 %copy-start.55 = (f32[2048,1]{0,1:T(1,128)}, f32[2048,1]{0,1:T(1,128)S(1)}, u32[]{:S(2)}) copy-start(f32[2048,1]{0,1:T(1,128)S(1)} %get-tuple-element.50) | copy-start | bytes 24580
  42.0 248.5 %copy-start.57 = (f32[2048,1]{0,1:T(1,128)}, f32[2048,1]{0,1:T(1,128)S(1)}, u32[]{:S(2)}) copy-start(f32[2048,1]{0,1:T(1,128)S(1)} %get-tuple-element.51) | copy-start | bytes 24580
  144.6 145.9 %copy-start.2 = (f32[384,2048]{1,0:T(8,128)}, f32[384,2048]{1,0:T(8,128)S(1)}, u32[]{:S(2)}) copy-start(f32[384,2048]{1,0:T(8,128)S(1)} %get-tuple-element.56) | copy-start | bytes 9437188
  269.9 20.6 copy-start
  269.9 20.6 copy-start.69
  297.1 268.0 %all-gather.8.cloned.1.call-start = ((), (), s32[]{:S(2)}) async-start(), calls=%async_computation.14 | async-start | bytes 7864320 | tf_op jit(solution)/shard_map/all_gather | solution.py:109
  297.2 27.6 collective-permute-start
  324.8 26.3 collective-permute-start.1
  351.0 25.3 collective-permute-start.2
  376.4 24.4 collective-permute-start.3
  401.8 23.6 collective-permute-start.4
  425.4 23.3 collective-permute-start.5
  426.7 22.2 copy-start.48
  448.7 21.9 collective-permute-start.6
  449.1 25.1 copy-start.19
  449.1 25.1 copy-start.81
  449.1 25.1 copy-start.89
  478.9 37.3 %copy-start.77 = (s32[1536]{0:T(1024)S(1)}, s32[1536]{0:T(1024)}, u32[]{:S(2)}) copy-start(s32[1536]{0:T(1024)} %copy-done.76) | copy-start | bytes 18436
  478.9 37.3 %copy-start.91 = (s32[384]{0:T(512)S(1)}, s32[384]{0:T(512)}, u32[]{:S(2)}) copy-start(s32[384]{0:T(512)} %get-tuple-element.27) | copy-start | bytes 4612
  478.9 37.7 %copy-start.29 = (bf16[1,384,2048]{2,1,0:T(8,128)(2,1)S(1)}, bf16[1,384,2048]{2,1,0:T(8,128)(2,1)}, u32[]{:S(2)}) copy-start(bf16[1,384,2048]{2,1,0:T(8,128)(2,1)} %param.23) | copy-start | bytes 4718596
  478.9 170.8 %all-gather.16.cloned.1.call-start = ((), (), s32[]{:S(2)}) async-start(), calls=%async_computation.18 | async-start | bytes 9437184 | tf_op jit(solution)/shard_map/all_gather | solution.py:80
  515.9 140.7 %copy-start.53 = (bf16[2048,16]{0,1:T(8,128)(2,1)}, bf16[2048,16]{0,1:T(8,128)(2,1)S(1)}, u32[]{:S(2)}) copy-start(bf16[2048,16]{0,1:T(8,128)(2,1)S(1)} %all_gather.35) | copy-start | bytes 196612
  516.6 48.6 %copy-start.6 = (pred[384,1536]{1,0:T(8,128)(4,1)}, pred[384,1536]{1,0:T(8,128)(4,1)S(1)}, u32[]{:S(2)}) copy-start(pred[384,1536]{1,0:T(8,128)(4,1)S(1)} %broadcast_compare_fusion) | copy-start | bytes 1769476
  518.6 188.8 %copy-start.74 = (s32[3072,1]{0,1:T(1,128)}, s32[3072,1]{0,1:T(1,128)S(1)}, u32[]{:S(2)}) copy-start(s32[3072,1]{0,1:T(1,128)S(1)} %compare_select_fusion) | copy-start | bytes 36868
  565.1 20.1 copy-start.50
  565.1 84.6 %copy-start.20 = (bf16[1,384,2048]{2,1,0:T(8,128)(2,1)S(1)}, bf16[1,384,2048]{2,1,0:T(8,128)(2,1)}, u32[]{:S(2)}) copy-start(bf16[1,384,2048]{2,1,0:T(8,128)(2,1)} %param.12) | copy-start | bytes 4718596
  659.4 28.4 copy-start.35
  701.2 345.9 %all-to-all-start.2 = ((bf16[16,240,2048]{2,1,0:T(8,128)(2,1)}), bf16[16,240,2048]{2,1,0:T(8,128)(2,1)}, u32[]{:S(2)}, u32[]{:S(2)}) async-start(bf16[16,240,2048]{2,1,0:T(8,128)(2,1)} %bitcast.209), calls=%async_computation.2 | async-start | bytes 31457280 | tf_op jit(solution)/shard_map/all_to_all | solution.py:180
  706.9 698.7 %all-gather.18.cloned.1.call-start = ((), (), s32[]{:S(2)}) async-start(), calls=%async_computation.19 | async-start | bytes 20971520 | tf_op jit(solution)/shard_map/all_gather | solution.py:152
  1047.1 345.0 %all-to-all-start = ((bf16[16,240,2048]{2,1,0:T(8,128)(2,1)}), bf16[16,240,2048]{2,1,0:T(8,128)(2,1)}, u32[]{:S(2)}, u32[]{:S(2)}) async-start(bf16[16,240,2048]{2,1,0:T(8,128)(2,1)} %bitcast.208), calls=%async_computation | async-start | bytes 31457280 | tf_op jit(solution)/shard_map/all_to_all | solution.py:150
  1052.7 397.6 %all-gather.20.cloned.1.call-start = ((), (), s32[]{:S(2)}) async-start(), calls=%async_computation.20 | async-start | bytes 10485760 | tf_op jit(solution)/shard_map/all_gather | solution.py:153
  1405.6 23.7 copy-start.17
  1535.9 344.4 %all-to-all-start.1 = ((bf16[2,1920,2048]{2,0,1:T(2,128)(2,1)}), bf16[2,1920,2048]{2,0,1:T(2,128)(2,1)}, u32[]{:S(2)}, u32[]{:S(2)}) async-start(bf16[2,1920,2048]{2,0,1:T(2,128)(2,1)} %copy.129), calls=%async_computation.1 | async-start | bytes 31457280 | tf_op jit(solution)/shard_map/all_to_all | solution.py:164
  1622.1 263.9 %copy-start.75 = (s32[3072,1]{0,1:T(1,128)S(1)}, s32[3072,1]{0,1:T(1,128)}, u32[]{:S(2)}) copy-start(s32[3072,1]{0,1:T(1,128)} %copy-done.74) | copy-start | bytes 36868
  1880.2 345.2 %all-to-all-start.3 = ((bf16[2,1920,2048]{2,0,1:T(2,128)(2,1)}), bf16[2,1920,2048]{2,0,1:T(2,128)(2,1)}, u32[]{:S(2)}, u32[]{:S(2)}) async-start(bf16[2,1920,2048]{2,0,1:T(2,128)(2,1)} %copy.133), calls=%async_computation.3 | async-start | bytes 31457280 | tf_op jit(solution)/shard_map/all_to_all | solution.py:216
  1885.9 571.2 %reduce-scatter.33.cloned.1.call-start = ((), (), s32[]{:S(2)}) async-start(), calls=%async_computation.29 | async-start | bytes 7864320
  1886.0 19.0 copy-start.63
  1905.0 31.5 copy-start.10
  1905.0 31.5 copy-start.36
  1936.5 13.2 copy-start.60
  1936.5 13.3 copy-start.68
  1951.3 335.4 %copy-start.65 = (bf16[384,16]{0,1:T(8,128)(2,1)}, bf16[384,16]{0,1:T(8,128)(2,1)S(1)}, u32[]{:S(2)}) copy-start(bf16[384,16]{0,1:T(8,128)(2,1)S(1)} %multiply_convert_fusion.6) | copy-start | bytes 36868
  2275.6 11.1 copy-start.62
  2275.6 11.1 copy-start.79
  2326.6 143.6 %reduce-scatter.31.cloned.1.call-start = ((), (), s32[]{:S(2)}) async-start(), calls=%async_computation.28 | async-start | bytes 7864320
  2358.6 32.2 copy-start.12
  2412.0 210.7 %reduce-scatter.23.cloned.1.call-start = ((), (), s32[]{:S(2)}) async-start(), calls=%async_computation.24 | async-start | bytes 9437184 | tf_op jit(solution)/shard_map/reduce_scatter | solution.py:313
  2422.6 352.3 %reduce-scatter.17.cloned.1.call-start = ((), (), s32[]{:S(2)}) async-start(), calls=%async_computation.21 | async-start | bytes 9437184 | tf_op jit(solution)/shard_map/reduce_scatter | solution.py:304
  2457.0 469.3 %reduce-scatter.21.cloned.1.call-start = ((), (), s32[]{:S(2)}) async-start(), calls=%async_computation.23 | async-start | bytes 9437184 | tf_op jit(solution)/shard_map/reduce_scatter | solution.py:310
  2466.8 611.7 %reduce-scatter.19.cloned.1.call-start = ((), (), s32[]{:S(2)}) async-start(), calls=%async_computation.22 | async-start | bytes 9437184 | tf_op jit(solution)/shard_map/reduce_scatter | solution.py:307
  2489.3 662.3 %reduce-scatter.29.cloned.1.call-start = ((), (), s32[]{:S(2)}) async-start(), calls=%async_computation.27 | async-start | bytes 10485760 | tf_op jit(solution)/shard_map/reduce_scatter | solution.py:212
  2513.5 766.9 %reduce-scatter.27.cloned.1.call-start = ((), (), s32[]{:S(2)}) async-start(), calls=%async_computation.26 | async-start | bytes 20971520 | tf_op jit(solution)/shard_map/reduce_scatter | solution.py:206
  2566.8 779.4 %reduce-scatter.35.cloned.1.call-start = ((), (), s32[]{:S(2)}) async-start(), calls=%async_computation.30 | async-start | bytes 589824
  2568.2 17.4 slice-start.2
  2594.4 808.3 %reduce-scatter.25.cloned.1.call-start = ((), (), s32[]{:S(2)}) async-start(), calls=%async_computation.25 | async-start | bytes 73728 | tf_op jit(solution)/shard_map/reduce_scatter | solution.py:316
  2595.5 895.0 %all-reduce.10.cloned.1.call-start = ((), (), s32[]{:S(2)}) async-start(), calls=%async_computation.31 | async-start | bytes 8388608 | tf_op jit(solution)/shard_map/psum | solution.py:324
  3155.6 131.2 %copy-start.84 = (f32[384]{0:T(512)S(1)}, f32[384]{0:T(512)}, u32[]{:S(2)}) copy-start(f32[384]{0:T(512)} %copy-done.83) | copy-start | bytes 4612
  (68 other events, 224.4 us)
Sparse Core Ops, SparseCore 0:
  10.2 127.7 all-gather.9
  140.1 123.1 all-gather.11
  297.2 44.5 all-gather.13
  479.0 43.6 all-gather.7
  524.7 124.9 all-gather.15
  709.0 109.4 all-gather.17
  1055.1 60.6 all-gather.19
  2326.7 58.2 reduce-scatter.32
  2412.1 58.0 reduce-scatter.30
  2473.7 149.0 reduce-scatter.22
  2626.8 147.9 reduce-scatter.16
  2778.3 147.9 reduce-scatter.20
  2930.4 147.9 reduce-scatter.18
  3080.9 70.7 reduce-scatter.28
  3154.3 126.0 reduce-scatter.26
  3284.2 61.9 reduce-scatter.34
  3350.0 52.6 reduce-scatter.24
  3405.3 85.1 all-reduce.9
